TPU v7x, 512 devices: a whole 4x8x8 slice. The times are simulated.
512 devices in a mesh: fsdp: 64 (over y, x, core), cent: 8 (over z).
Axes of the slice: x: 4, y: 8, z: 8, core: 2. Of those that a mesh axis runs over, the one named last changes fastest.
Arguments:
- attention: bfloat16 [8192, 4096], P('fsdp', 'cent'), may hold values from -6 to 6
- w_out: bfloat16 [4096, 4096], P('cent', 'fsdp'), may hold values from -0.09375 to 0.09375
- hidden: bfloat16 [8192, 4096], P(('fsdp', 'cent')), may hold values from -6 to 6
- norm_gain: bfloat16 [4096], replicated, may hold values from 0.099609375 to 1.8984375
- centroids: bfloat16 [512, 4096], P('cent'), may hold values from -3 to 3
- token_codes: int32 [8192], P(('fsdp', 'cent')), may hold values from 0 to 63, as said below
- tile_lists: int32 [64, 8], P('fsdp'), may hold values from 0 to 63, as said below
Outputs:
- centroid_sums: float32 [512, 4096], P('cent', 'fsdp')
- residual_gram: float32 [4096, 4096], P('fsdp', 'cent')
Inputs may be any that keep to these rules, and one draw needn't show every extreme that they name: `token_codes`: token t belongs to block t // 128; its code k names centroid k % 8 of the tile at slot k // 8 of that block's list; every slot of a block's list is used. `tile_lists`: each row holds 8 distinct tile ids in ascending order; tile j holds centroids j * 8 to j * 8 + 7, and centroid g belongs to owner shard g // 64; in every row at most 2 listed tiles share an owner, and exactly 2 do for some owner.
All inputs are finite; a program needn't handle non-finite values.
Results may differ from a plain program's by a relative error of at most 0.0085.
Values may be sent and summed in bfloat16 or wider, within the bound.
A program may use at most 64 MiB of HBM per device.

v0:
```python
import jax
import jax.numpy as jnp
from jax import lax
from jax.sharding import PartitionSpec as P

TILE = 8
LT = 8


def shards(attention, w_out, hidden, norm_gain, centroids, token_codes, tile_lists):
    tok_dev = hidden.shape[0]
    feat_dim = hidden.shape[1]
    n_fsdp = lax.axis_size("fsdp")
    n_cent = lax.axis_size("cent")
    cap_slots = max(2, 2 * LT // n_cent)
    partial_out = jnp.dot(
        attention,
        lax.all_gather(w_out, "fsdp", axis=1, tiled=True),
        preferred_element_type=jnp.float32,
    )
    head_sum = lax.psum_scatter(
        partial_out.astype(jnp.bfloat16), "cent", scatter_dimension=0, tiled=True
    ).astype(jnp.float32)
    mixed_rows = hidden.astype(jnp.float32) + head_sum
    normed = (
        mixed_rows
        * lax.rsqrt(jnp.mean(mixed_rows * mixed_rows, axis=1, keepdims=True) + 1e-05)
        * norm_gain.astype(jnp.float32)
    )
    cent_dev = centroids.shape[0]
    own_tiles = cent_dev // TILE
    owner_idx = lax.axis_index("cent")
    listed = tile_lists[0]
    local_tile = listed - owner_idx * own_tiles
    owned_here = (local_tile >= 0) & (local_tile < own_tiles)
    safe_tile = jnp.clip(local_tile, 0, own_tiles - 1)
    tiles_here = centroids.reshape(own_tiles, TILE, feat_dim)
    slot_of = token_codes // TILE
    offset = token_codes % TILE
    rank_mine = jnp.cumsum(owned_here.astype(jnp.int32)) - 1
    chosen = owned_here[None, :] & (
        rank_mine[None, :] == jnp.arange(cap_slots, dtype=jnp.int32)[:, None]
    )
    send_tile = jnp.sum(jnp.where(chosen, safe_tile[None, :], 0), axis=1)
    filled = jnp.any(chosen, axis=1)
    outgoing = jnp.where(
        filled[:, None, None],
        jnp.take(tiles_here, send_tile, axis=0),
        jnp.zeros((cap_slots, TILE, feat_dim), jnp.bfloat16),
    )
    arrived = lax.all_gather(outgoing, "cent", axis=0, tiled=True)
    owner_of = listed // own_tiles
    list_pos = jnp.arange(LT, dtype=jnp.int32)
    earlier = (owner_of[None, :] == owner_of[:, None]) & (list_pos[None, :] < list_pos[:, None])
    rank_all = jnp.sum(earlier.astype(jnp.int32), axis=1)
    where_tile = owner_of * cap_slots + rank_all
    tile_rows = arrived.reshape(-1, feat_dim)
    centers = jnp.take(tile_rows, where_tile[slot_of] * TILE + offset, axis=0)
    residual = (normed - centers.astype(jnp.float32)).astype(jnp.bfloat16)
    onehot = (token_codes[None, :] == jnp.arange(LT * TILE, dtype=jnp.int32)[:, None]).astype(
        jnp.bfloat16
    )
    slot_part = jnp.dot(onehot, residual, preferred_element_type=jnp.float32)
    slot_sum = lax.psum(slot_part.astype(jnp.bfloat16), "cent").astype(jnp.float32)
    target = (local_tile[:, None] * TILE + jnp.arange(TILE, dtype=jnp.int32)[None, :]).reshape(-1)
    valid_rows = jnp.repeat(owned_here, TILE)
    placer = (
        (jnp.arange(cent_dev, dtype=jnp.int32)[:, None] == target[None, :]) & valid_rows[None, :]
    ).astype(jnp.float32)
    dense_part = jnp.dot(
        placer, slot_sum, precision=lax.Precision.HIGHEST, preferred_element_type=jnp.float32
    )
    centroid_sums = lax.psum_scatter(dense_part, "fsdp", scatter_dimension=1, tiled=True)
    rows_dev = feat_dim // n_fsdp
    row_start = lax.axis_index("fsdp") * rows_dev
    shard_rows = lax.all_gather(residual, "fsdp", axis=0, tiled=True)
    left_cols = lax.dynamic_slice_in_dim(shard_rows, row_start, rows_dev, 1)
    gram_part = lax.dot_general(
        left_cols, shard_rows, (((0,), (0,)), ((), ())), preferred_element_type=jnp.float32
    )
    gram_sum = lax.psum_scatter(gram_part, "cent", scatter_dimension=1, tiled=True)
    tokens_all = tok_dev * n_fsdp * n_cent
    return (centroid_sums, gram_sum / tokens_all)


def solution(mesh):
    in_specs = (
        P("fsdp", "cent"),
        P("cent", "fsdp"),
        P(("fsdp", "cent"), None),
        P(),
        P("cent", None),
        P(("fsdp", "cent")),
        P("fsdp", None),
    )
    out_specs = (P("cent", "fsdp"), P("fsdp", "cent"))
    return jax.shard_map(shards, mesh=mesh, in_specs=in_specs, out_specs=out_specs, check_vma=False)
```

profile of v0, /device:TPU:2, one launch (start us, length us, event | category | flops | bytes accessed | tf_op | source)
XLA Modules:
  0.0 561.0 jit_solution(6380447563696765636)
XLA Ops:
  7.2 0.0 copy-start
  7.2 0.0 copy-start.4
  7.2 0.0 copy-start.3
  7.2 0.0 copy-start.5
  7.2 0.0 all-gather.4.cloned.1.call-start
  7.3 0.7 all-gather.4.cloned.1.call-update
  7.9 0.0 all-gather.6.cloned.1.call-start
  8.0 0.7 convert_bitcast_fusion
  8.7 0.2 reduce-window.8
  8.9 0.7 fusion.11
  9.5 0.1 select_reduce_fusion
  9.7 0.0 copy-done
  9.7 0.6 gather_fusion.1
  10.2 0.1 fusion.8
  10.4 0.7 select_select_fusion
  11.1 0.0 copy-start.2
  11.1 0.0 all-gather.6.cloned.1.call-update
  11.1 0.0 reduce-scatter.6.cloned.1.call-start
  11.2 88.0 %all-gather.4.cloned.1.call-done = bf16[512,4096]{0,1:T(8,128)(2,1)} async-done(((bf16[512,64]{0,1:T(8,128)(2,1)}), bf16[512,4096]{0,1:T(8,128)(2,1)}) %all-gather.4.cloned.1.call-update) | async-done | bytes 4194320 | tf_op jit(solution)/shard_map/all_gather | solution.py:18
  99.2 4.8 convolution_convert_fusion
  104.0 0.0 reduce-scatter.6.cloned.1.call-update
  104.0 0.0 all-reduce.2.cloned.1.call-start
  104.1 0.0 copy-done.3
  104.1 0.0 copy-done.5
  104.1 0.0 copy-done.4
  104.1 0.2 convert_reduce_fusion
  104.3 0.7 gather_fusion
  105.0 37.3 %all-gather.6.cloned.1.call-done = bf16[16,8,4096]{2,1,0:T(8,128)(2,1)} async-done(((bf16[2,8,4096]{2,1,0:T(8,128)(2,1)}), bf16[16,8,4096]{2,1,0:T(8,128)(2,1)}) %all-gather.6.cloned.1.call-update) | async-done | bytes 1048592 | tf_op jit(solution)/shard_map/all_gather | solution.py:51
  142.4 2.1 gather_fusion.2
  144.5 41.3 %reduce-scatter.6.cloned.1.call-done = bf16[16,4096]{1,0:T(8,128)(2,1)} async-done(((bf16[128,4096]{1,0:T(8,128)(2,1)}), bf16[16,4096]{1,0:T(8,128)(2,1)}) %reduce-scatter.6.cloned.1.call-update) | async-done | bytes 131088 | tf_op jit(solution)/shard_map/reduce_scatter | solution.py:21
  185.8 0.0 copy-done.2
  185.8 1.1 multiply_reduce_fusion
  186.9 1.0 subtract_convert_fusion
  187.9 0.0 copy-start.1
  187.9 1.1 convolution_convert_fusion.1
  189.1 0.0 all-reduce.2.cloned.1.call-update
  189.1 0.0 all-gather.8.cloned.1.call-start
  189.1 0.0 copy-done.1
  189.1 0.5 all-gather.8.cloned.1.call-update
  189.7 0.0 reduce-scatter.10.cloned.1.call-start
  189.7 0.1 iota_add_fusion
  189.8 0.1 add.94
  189.9 0.1 broadcast_in_dim.69
  190.0 0.1 and.75
  190.1 77.2 %all-reduce.2.cloned.1.call-done = bf16[64,4096]{1,0:T(8,128)(2,1)} async-done(((bf16[64,4096]{1,0:T(8,128)(2,1)}), bf16[64,4096]{1,0:T(8,128)(2,1)}) %all-reduce.2.cloned.1.call-update) | async-done | bytes 524304 | tf_op jit(solution)/shard_map/psum | solution.py:64
  267.3 2.9 convolution_bitcast_fusion
  270.2 0.0 reduce-scatter.10.cloned.1.call-update
  270.2 0.0 reduce-scatter.8.cloned.1.call-start
  270.3 85.8 %all-gather.8.cloned.1.call-done = bf16[1024,4096]{1,0:T(8,128)(2,1)} async-done(((bf16[16,4096]{1,0:T(8,128)(2,1)}), bf16[1024,4096]{1,0:T(8,128)(2,1)}) %all-gather.8.cloned.1.call-update) | async-done | bytes 8388624 | tf_op jit(solution)/shard_map/all_gather | solution.py:76
  356.1 6.1 %fusion = f32[64,4096]{1,0:T(8,128)} fusion(bf16[1024,4096]{1,0:T(8,128)(2,1)} %all-gather.8.cloned.1.call-done, s32[]{:T(128)S(6)} %select_n.78), kind=kOutput, calls=%fused_computation.6 | convolution fusion | flops 536870912 | bytes 9699332 | tf_op jit(solution)/shard_map/dot_general | solution.py:78
  362.3 0.0 reduce-scatter.8.cloned.1.call-update
  362.3 145.4 %reduce-scatter.10.cloned.1.call-done = f32[64,64]{1,0:T(8,128)} async-done(((f32[4096,64]{1,0:T(8,128)}), f32[64,64]{1,0:T(8,128)}) %reduce-scatter.10.cloned.1.call-update) | async-done | bytes 16400
  507.7 1.5 copy.10
  509.1 43.5 %reduce-scatter.8.cloned.1.call-done = f32[64,512]{1,0:T(8,128)} async-done(((f32[64,4096]{1,0:T(8,128)}), f32[64,512]{1,0:T(8,128)}) %reduce-scatter.8.cloned.1.call-update) | async-done | bytes 131088 | tf_op jit(solution)/shard_map/reduce_scatter | solution.py:81
  552.6 1.6 broadcast_multiply_fusion
  (13 shorter events, 0.1 us)
Async XLA Ops:
  7.2 2.5 copy-start
  7.2 96.9 %copy-start.4 = (s32[1,8]{1,0:T(1,128)S(1)}, s32[1,8]{1,0:T(1,128)}, u32[]{:S(2)}) copy-start(s32[1,8]{1,0:T(1,128)} %param.13) | copy-start | bytes 100
  7.2 96.9 %copy-start.3 = (bf16[4096]{0:T(1024)(128)(2,1)S(1)}, bf16[4096]{0:T(1024)(128)(2,1)}, u32[]{:S(2)}) copy-start(bf16[4096]{0:T(1024)(128)(2,1)} %param.10) | copy-start | bytes 24580
  7.2 96.9 %copy-start.5 = (s32[16]{0:T(128)S(1)}, s32[16]{0:T(128)}, u32[]{:S(2)}) copy-start(s32[16]{0:T(128)} %param.12) | copy-start | bytes 196
  7.2 92.0 %all-gather.4.cloned.1.call-start = ((), (), s32[]{:S(2)}) async-start(), calls=%async_computation.3 | async-start | bytes 4259840 | tf_op jit(solution)/shard_map/all_gather | solution.py:18
  7.9 134.4 %all-gather.6.cloned.1.call-start = ((), (), s32[]{:S(2)}) async-start(), calls=%async_computation.5 | async-start | bytes 1179648 | tf_op jit(solution)/shard_map/all_gather | solution.py:51
  11.1 174.7 %copy-start.2 = (bf16[16,4096]{1,0:T(8,128)(2,1)S(1)}, bf16[16,4096]{1,0:T(8,128)(2,1)}, u32[]{:S(2)}) copy-start(bf16[16,4096]{1,0:T(8,128)(2,1)} %param.9) | copy-start | bytes 393220
  11.1 174.7 %reduce-scatter.6.cloned.1.call-start = ((), (), s32[]{:S(2)}) async-start(), calls=%async_computation.4 | async-start | bytes 1179648 | tf_op jit(solution)/shard_map/reduce_scatter | solution.py:21
  104.0 163.3 %all-reduce.2.cloned.1.call-start = ((), (), s32[]{:S(2)}) async-start(), calls=%async_computation.6 | async-start | bytes 1048576 | tf_op jit(solution)/shard_map/psum | solution.py:64
  187.9 1.2 copy-start.1
  189.1 167.0 %all-gather.8.cloned.1.call-start = ((), (), s32[]{:S(2)}) async-start(), calls=%async_computation.7 | async-start | bytes 8519680 | tf_op jit(solution)/shard_map/all_gather | solution.py:76
  189.7 318.0 %reduce-scatter.10.cloned.1.call-start = ((), (), s32[]{:S(2)}) async-start(), calls=%async_computation.9 | async-start | bytes 2129920
  270.2 282.3 %reduce-scatter.8.cloned.1.call-start = ((), (), s32[]{:S(2)}) async-start(), calls=%async_computation.8 | async-start | bytes 1179648 | tf_op jit(solution)/shard_map/reduce_scatter | solution.py:81
Sparse Core Ops, SparseCore 0:
  11.4 87.8 all-gather.3
  101.9 40.4 all-gather.5
  145.2 40.5 reduce-scatter.5
  189.2 78.0 all-reduce.1
  271.1 84.9 all-gather.7
  360.6 147.0 reduce-scatter.9
  510.5 42.0 reduce-scatter.7
where the time goes:
time: 561 us
  waiting for transfers between devices  520 us (93%)
  matrix products  15 us (3%)
  between operations  14.3 us (3%)
  other arithmetic  6.51 us (1%)
    unnamed x8, waiting for transfers between devices  147 us
    all_gather x1, waiting for transfers between devices, shards(): lax.all_gather(w_out, 'fsdp', axis=1, tiled=True)  88 us
    all_gather x1, waiting for transfers between devices, shards(): shard_rows = lax.all_gather(residual, 'fsdp', axis=0, tiled=True)  85.8 us
    psum x1, waiting for transfers between devices, shards(): lax.psum(slot_part.astype(jnp.bfloat16), 'cent').astype(jnp.float32)  77.2 us
    reduce_scatter x1, waiting for transfers between devices, shards(): lax.psum_scatter(gram_part, 'cent', scatter_dimension=1, tiled=True)  43.5 us
    reduce_scatter x1, waiting for transfers between devices, shards(): lax.psum_scatter(partial_out.astype(jnp.bfloat16), 'cent', scatter_dimens...  41.3 us
    all_gather x1, waiting for transfers between devices, shards(): arrived = lax.all_gather(outgoing, 'cent', axis=0, tiled=True)  37.3 us
  transfers between devices with their start and end apart: 7, of which 7 were waited for; matrix products, arithmetic and copies ran while one was open for 4% of the time, Pallas kernels for 0%

commit v1 on v0

--- a/solution.py
+++ b/solution.py
@@ -2,9 +2,39 @@
 import jax.numpy as jnp
 from jax import lax
 from jax.sharding import PartitionSpec as P
+from jax.lax import axis_index, axis_size, ppermute
 
 TILE = 8
 LT = 8
+
+
+def move_the_side(base_x, ax_name):
+    new, mat_out, f_next = (axis_size(ax_name), axis_index(ax_name), base_x.shape[0])
+    left_arr = e_next = base_x
+    step_out = lax.dynamic_update_slice_in_dim(
+        jnp.zeros(
+            tuple((nth * new if s == 0 else nth for s, nth in enumerate(base_x.shape))),
+            base_x.dtype,
+        ),
+        base_x,
+        mat_out * f_next,
+        axis=0,
+    )
+    for rr in range(1, new // 2 + 1):
+        left_arr = ppermute(
+            left_arr, axis_name=ax_name, perm=tuple(((s, (s + 1) % new) for s in range(new)))
+        )
+        step_out = lax.dynamic_update_slice_in_dim(
+            step_out, left_arr, (mat_out - rr) % new * f_next, axis=0
+        )
+        if 2 * rr < new:
+            e_next = ppermute(
+                e_next, axis_name=ax_name, perm=tuple(((s, (s - 1) % new) for s in range(new)))
+            )
+            step_out = lax.dynamic_update_slice_in_dim(
+                step_out, e_next, (mat_out + rr) % new * f_next, axis=0
+            )
+    return step_out
 
 
 def shards(attention, w_out, hidden, norm_gain, centroids, token_codes, tile_lists):
@@ -48,7 +78,7 @@
         jnp.take(tiles_here, send_tile, axis=0),
         jnp.zeros((cap_slots, TILE, feat_dim), jnp.bfloat16),
     )
-    arrived = lax.all_gather(outgoing, "cent", axis=0, tiled=True)
+    arrived = move_the_side(outgoing, "cent")
     owner_of = listed // own_tiles
     list_pos = jnp.arange(LT, dtype=jnp.int32)
     earlier = (owner_of[None, :] == owner_of[:, None]) & (list_pos[None, :] < list_pos[:, None])

time: 561 us -> 521 us (0.929)
  waiting for transfers between devices: 520 us -> 448 us
  starting transfers between devices: 0.28 us -> 30.8 us
    all_gather x1 -> x0, waiting for transfers between devices: 37.3 us -> none  [shards(): arrived = lax.all_gather(outgoing, 'cent', axis=0, tiled=True)]
    all_gather x1, waiting for transfers between devices: 88 us -> 56.9 us  [shards(): lax.all_gather(w_out, 'fsdp', axis=1, tiled=True)]
    ppermute x0 -> x7, starting transfers between devices: none -> 30.5 us  [the longest x3 18.9 us: move_the_side(): ppermute(e_next, axis_name=ax_name, perm=tuple(((s, (s - 1) % new) for s...]
    reduce_scatter x1, waiting for transfers between devices: 41.3 us -> 30.7 us  [shards(): lax.psum_scatter(partial_out.astype(jnp.bfloat16), 'cent', scatter_dimens...]
    ppermute x0 -> x7, waiting for transfers between devices: none -> 7.04 us  [the longest x4 7.03 us: move_the_side(): ppermute(left_arr, axis_name=ax_name, perm=tuple(((s, (s + 1) % new) for...]
    unnamed x8 -> x7, waiting for transfers between devices: 147 us -> 147 us
  transfers between devices with their start and end apart: 7 -> 13, of which waited for: 7 -> 8; matrix products, arithmetic and copies ran while one was open for 4% -> 4% of each run, Pallas kernels for 0% -> 0%
where the time goes in v1:
time: 521 us; the launch traced here: 520 us
  waiting for transfers between devices  448 us (86%)
  starting transfers between devices  30.8 us (6%)
  matrix products  14.9 us (3%)
  between operations  14.5 us (3%)
  other arithmetic  8.54 us (2%)
    unnamed x7, waiting for transfers between devices  147 us
    all_gather x1, waiting for transfers between devices, shards(): shard_rows = lax.all_gather(residual, 'fsdp', axis=0, tiled=True)  85.8 us
    psum x1, waiting for transfers between devices, shards(): lax.psum(slot_part.astype(jnp.bfloat16), 'cent').astype(jnp.float32)  77.2 us
    all_gather x1, waiting for transfers between devices, shards(): lax.all_gather(w_out, 'fsdp', axis=1, tiled=True)  56.9 us
    reduce_scatter x1, waiting for transfers between devices, shards(): lax.psum_scatter(gram_part, 'cent', scatter_dimension=1, tiled=True)  43.4 us
    reduce_scatter x1, waiting for transfers between devices, shards(): lax.psum_scatter(partial_out.astype(jnp.bfloat16), 'cent', scatter_dimens...  30.7 us
    ppermute x3, starting transfers between devices, move_the_side(): ppermute(e_next, axis_name=ax_name, perm=tuple(((s, (s - 1) % new) for s...  18.9 us
    ppermute x4, starting transfers between devices, move_the_side(): ppermute(left_arr, axis_name=ax_name, perm=tuple(((s, (s + 1) % new) for...  11.7 us
  transfers between devices with their start and end apart: 13, of which 8 were waited for; matrix products, arithmetic and copies ran while one was open for 4% of the time, Pallas kernels for 0%

profile of v1, /device:TPU:2, one launch (start us, length us, event | category | flops | bytes accessed | tf_op | source)
XLA Modules:
  0.0 520.2 jit_solution(4463569754238815156)
XLA Ops:
  7.2 0.0 copy-start
  7.2 0.0 all-gather.3.cloned.1.call-start
  7.2 0.7 all-gather.3.cloned.1.call-update
  7.9 0.0 reduce-scatter.6.cloned.1.call-start
  8.0 0.7 convert_bitcast_fusion
  8.6 0.2 reduce-window.8
  8.8 0.7 fusion.12
  9.5 0.1 select_reduce_fusion
  9.6 0.6 gather_fusion.1
  10.2 0.1 fusion.9
  10.3 0.1 broadcast_in_dim.75
  10.4 0.1 constant_dynamic-update-slice_fusion.7
  10.5 4.3 collective-permute-start
  14.8 8.6 %collective-permute-start.1 = (bf16[2,8,4096]{2,1,0:T(8,128)(2,1)S(1)}, bf16[2,8,4096]{2,1,0:T(8,128)(2,1)S(1)}, u32[]{:S(2)}, u32[]{:S(2)}) collective-permute-start(bf16[2,8,4096]{2,1,0:T(8,128)(2,1)S(1)} %get-tuple-element.5), channel_id=1, source_target_pairs={{0,7},{1,0},{2,1},{3,2},{4,3},{5,4},{6,5},{7,6},{8,15},{9,8},{10,9... | collective-permute-start | bytes 393224 | tf_op jit(solution)/shard_map/ppermute | solution.py:31
  23.4 0.7 compare_select_fusion.3
  24.1 0.7 fusion.13
  24.8 0.2 convert_reduce_fusion
  24.9 0.7 gather_fusion
  25.6 0.7 compare_and_fusion.3
  26.4 0.7 convert_element_type.35
  27.1 0.0 collective-permute-done
  27.1 1.9 collective-permute-start.2
  29.0 0.0 collective-permute-done.1
  29.1 5.1 collective-permute-start.3
  34.2 0.0 copy-start.2
  34.3 0.0 copy-start.4
  34.3 0.0 copy-start.3
  34.3 0.9 collective-permute-done.2
  35.2 1.9 collective-permute-start.4
  37.1 0.0 collective-permute-done.3
  37.1 5.1 collective-permute-start.5
  42.3 56.9 %all-gather.3.cloned.1.call-done = bf16[512,4096]{0,1:T(8,128)(2,1)} async-done(((bf16[512,64]{0,1:T(8,128)(2,1)}), bf16[512,4096]{0,1:T(8,128)(2,1)}) %all-gather.3.cloned.1.call-update) | async-done | bytes 4194320 | tf_op jit(solution)/shard_map/all_gather | solution.py:48
  99.2 4.7 convolution_convert_fusion
  103.9 0.0 reduce-scatter.6.cloned.1.call-update
  103.9 0.0 all-reduce.2.cloned.1.call-start
  104.0 0.0 collective-permute-done.4
  104.0 3.6 collective-permute-start.6
  107.6 0.0 collective-permute-done.5
  107.7 6.1 %collective-permute-done.6 = bf16[2,8,4096]{2,1,0:T(8,128)(2,1)S(1)} collective-permute-done((bf16[2,8,4096]{2,1,0:T(8,128)(2,1)S(1)}, bf16[2,8,4096]{2,1,0:T(8,128)(2,1)S(1)}, u32[]{:S(2)}, u32[]{:S(2)}) %collective-permute-start.6) | collective-permute-done | bytes 131104 | tf_op jit(solution)/shard_map/ppermute | solution.py:24
  113.8 0.6 gather_fusion.2
  114.4 30.7 %reduce-scatter.6.cloned.1.call-done = bf16[16,4096]{1,0:T(8,128)(2,1)} async-done(((bf16[128,4096]{1,0:T(8,128)(2,1)}), bf16[16,4096]{1,0:T(8,128)(2,1)}) %reduce-scatter.6.cloned.1.call-update) | async-done | bytes 131088 | tf_op jit(solution)/shard_map/reduce_scatter | solution.py:51
  145.1 1.1 multiply_reduce_fusion
  146.2 1.0 subtract_convert_fusion
  147.2 0.0 copy-start.1
  147.2 1.1 convolution_convert_fusion.1
  148.3 0.0 all-reduce.2.cloned.1.call-update
  148.4 0.0 all-gather.5.cloned.1.call-start
  148.4 0.5 all-gather.5.cloned.1.call-update
  149.0 0.0 reduce-scatter.10.cloned.1.call-start
  149.0 0.1 iota_add_fusion
  149.1 0.1 add.153
  149.2 0.1 broadcast_in_dim.72
  149.2 0.1 and.104
  149.3 77.2 %all-reduce.2.cloned.1.call-done = bf16[64,4096]{1,0:T(8,128)(2,1)} async-done(((bf16[64,4096]{1,0:T(8,128)(2,1)}), bf16[64,4096]{1,0:T(8,128)(2,1)}) %all-reduce.2.cloned.1.call-update) | async-done | bytes 524304 | tf_op jit(solution)/shard_map/psum | solution.py:94
  226.6 2.9 convolution_bitcast_fusion
  229.5 0.0 reduce-scatter.10.cloned.1.call-update
  229.5 0.0 reduce-scatter.8.cloned.1.call-start
  229.6 85.8 %all-gather.5.cloned.1.call-done = bf16[1024,4096]{1,0:T(8,128)(2,1)} async-done(((bf16[16,4096]{1,0:T(8,128)(2,1)}), bf16[1024,4096]{1,0:T(8,128)(2,1)}) %all-gather.5.cloned.1.call-update) | async-done | bytes 8388624 | tf_op jit(solution)/shard_map/all_gather | solution.py:106
  315.4 6.2 %fusion = f32[64,4096]{1,0:T(8,128)} fusion(bf16[1024,4096]{1,0:T(8,128)(2,1)} %all-gather.5.cloned.1.call-done, s32[]{:T(128)S(6)} %select_n.147), kind=kOutput, calls=%fused_computation.6 | convolution fusion | flops 536870912 | bytes 9699332 | tf_op jit(solution)/shard_map/dot_general | solution.py:108
  321.5 0.0 reduce-scatter.8.cloned.1.call-update
  321.6 145.4 %reduce-scatter.10.cloned.1.call-done = f32[64,64]{1,0:T(8,128)} async-done(((f32[4096,64]{1,0:T(8,128)}), f32[64,64]{1,0:T(8,128)}) %reduce-scatter.10.cloned.1.call-update) | async-done | bytes 16400
  466.9 1.5 copy.10
  468.4 43.4 %reduce-scatter.8.cloned.1.call-done = f32[64,512]{1,0:T(8,128)} async-done(((f32[64,4096]{1,0:T(8,128)}), f32[64,512]{1,0:T(8,128)}) %reduce-scatter.8.cloned.1.call-update) | async-done | bytes 131088 | tf_op jit(solution)/shard_map/reduce_scatter | solution.py:111
  511.7 1.6 broadcast_multiply_fusion
  (21 shorter events, 0.2 us)
Async XLA Ops:
  7.2 2.5 copy-start
  7.2 92.0 %all-gather.3.cloned.1.call-start = ((), (), s32[]{:S(2)}) async-start(), calls=%async_computation.3 | async-start | bytes 4259840 | tf_op jit(solution)/shard_map/all_gather | solution.py:48
  7.9 137.2 %reduce-scatter.6.cloned.1.call-start = ((), (), s32[]{:S(2)}) async-start(), calls=%async_computation.4 | async-start | bytes 1179648 | tf_op jit(solution)/shard_map/reduce_scatter | solution.py:51
  10.5 16.6 %collective-permute-start = (bf16[2,8,4096]{2,1,0:T(8,128)(2,1)S(1)}, bf16[2,8,4096]{2,1,0:T(8,128)(2,1)S(1)}, u32[]{:S(2)}, u32[]{:S(2)}) collective-permute-start(bf16[2,8,4096]{2,1,0:T(8,128)(2,1)S(1)} %get-tuple-element.5), channel_id=1, source_target_pairs={{0,1},{1,2},{2,3},{3,4},{4,5},{5,6},{6,7},{7,0},{8,9},{9,10},{10,1... | collective-permute-start | bytes 393224 | tf_op jit(solution)/shard_map/ppermute | solution.py:24
  14.8 14.2 %collective-permute-start.1 = (bf16[2,8,4096]{2,1,0:T(8,128)(2,1)S(1)}, bf16[2,8,4096]{2,1,0:T(8,128)(2,1)S(1)}, u32[]{:S(2)}, u32[]{:S(2)}) collective-permute-start(bf16[2,8,4096]{2,1,0:T(8,128)(2,1)S(1)} %get-tuple-element.5), channel_id=1, source_target_pairs={{0,7},{1,0},{2,1},{3,2},{4,3},{5,4},{6,5},{7,6},{8,15},{9,8},{10,9... | collective-permute-start | bytes 393224 | tf_op jit(solution)/shard_map/ppermute | solution.py:31
  27.1 8.1 %collective-permute-start.2 = (bf16[2,8,4096]{2,1,0:T(8,128)(2,1)S(1)}, bf16[2,8,4096]{2,1,0:T(8,128)(2,1)S(1)}, u32[]{:S(2)}, u32[]{:S(2)}) collective-permute-start(bf16[2,8,4096]{2,1,0:T(8,128)(2,1)S(1)} %collective-permute-done), channel_id=1, source_target_pairs={{0,1},{1,2},{2,3},{3,4},{4,5},{5,6},{6,7},{7,0},{8,9},{9,10},{10,1... | collective-permute-start | bytes 393224 | tf_op jit(solution)/shard_map/ppermute | solution.py:24
  29.1 8.1 %collective-permute-start.3 = (bf16[2,8,4096]{2,1,0:T(8,128)(2,1)S(1)}, bf16[2,8,4096]{2,1,0:T(8,128)(2,1)S(1)}, u32[]{:S(2)}, u32[]{:S(2)}) collective-permute-start(bf16[2,8,4096]{2,1,0:T(8,128)(2,1)S(1)} %collective-permute-done.1), channel_id=1, source_target_pairs={{0,7},{1,0},{2,1},{3,2},{4,3},{5,4},{6,5},{7,6},{8,15},{9,8},{10,9... | collective-permute-start | bytes 393224 | tf_op jit(solution)/shard_map/ppermute | solution.py:31
  34.2 110.9 %copy-start.2 = (bf16[16,4096]{1,0:T(8,128)(2,1)S(1)}, bf16[16,4096]{1,0:T(8,128)(2,1)}, u32[]{:S(2)}) copy-start(bf16[16,4096]{1,0:T(8,128)(2,1)} %param.9) | copy-start | bytes 393220
  34.3 113.0 %copy-start.4 = (s32[16]{0:T(128)S(1)}, s32[16]{0:T(128)}, u32[]{:S(2)}) copy-start(s32[16]{0:T(128)} %param.12) | copy-start | bytes 196
  34.3 114.9 %copy-start.3 = (s32[1,8]{1,0:T(1,128)S(1)}, s32[1,8]{1,0:T(1,128)}, u32[]{:S(2)}) copy-start(s32[1,8]{1,0:T(1,128)} %param.13) | copy-start | bytes 100
  35.2 68.8 %collective-permute-start.4 = (bf16[2,8,4096]{2,1,0:T(8,128)(2,1)S(1)}, bf16[2,8,4096]{2,1,0:T(8,128)(2,1)S(1)}, u32[]{:S(2)}, u32[]{:S(2)}) collective-permute-start(bf16[2,8,4096]{2,1,0:T(8,128)(2,1)S(1)} %collective-permute-done.2), channel_id=1, source_target_pairs={{0,1},{1,2},{2,3},{3,4},{4,5},{5,6},{6,7},{7,0},{8,9},{9,10},{10,1... | collective-permute-start | bytes 393224 | tf_op jit(solution)/shard_map/ppermute | solution.py:24
  37.1 70.5 %collective-permute-start.5 = (bf16[2,8,4096]{2,1,0:T(8,128)(2,1)S(1)}, bf16[2,8,4096]{2,1,0:T(8,128)(2,1)S(1)}, u32[]{:S(2)}, u32[]{:S(2)}) collective-permute-start(bf16[2,8,4096]{2,1,0:T(8,128)(2,1)S(1)} %collective-permute-done.3), channel_id=1, source_target_pairs={{0,7},{1,0},{2,1},{3,2},{4,3},{5,4},{6,5},{7,6},{8,15},{9,8},{10,9... | collective-permute-start | bytes 393224 | tf_op jit(solution)/shard_map/ppermute | solution.py:31
  103.9 122.7 %all-reduce.2.cloned.1.call-start = ((), (), s32[]{:S(2)}) async-start(), calls=%async_computation.5 | async-start | bytes 1048576 | tf_op jit(solution)/shard_map/psum | solution.py:94
  104.0 9.8 %collective-permute-start.6 = (bf16[2,8,4096]{2,1,0:T(8,128)(2,1)S(1)}, bf16[2,8,4096]{2,1,0:T(8,128)(2,1)S(1)}, u32[]{:S(2)}, u32[]{:S(2)}) collective-permute-start(bf16[2,8,4096]{2,1,0:T(8,128)(2,1)S(1)} %collective-permute-done.4), channel_id=1, source_target_pairs={{0,1},{1,2},{2,3},{3,4},{4,5},{5,6},{6,7},{7,0},{8,9},{9,10},{10,1... | collective-permute-start | bytes 393224 | tf_op jit(solution)/shard_map/ppermute | solution.py:24
  147.2 1.2 copy-start.1
  148.4 167.0 %all-gather.5.cloned.1.call-start = ((), (), s32[]{:S(2)}) async-start(), calls=%async_computation.6 | async-start | bytes 8519680 | tf_op jit(solution)/shard_map/all_gather | solution.py:106
  149.0 318.0 %reduce-scatter.10.cloned.1.call-start = ((), (), s32[]{:S(2)}) async-start(), calls=%async_computation.8 | async-start | bytes 2129920
  229.5 282.2 %reduce-scatter.8.cloned.1.call-start = ((), (), s32[]{:S(2)}) async-start(), calls=%async_computation.7 | async-start | bytes 1179648 | tf_op jit(solution)/shard_map/reduce_scatter | solution.py:111
Sparse Core Ops, SparseCore 0:
  11.3 87.7 all-gather.2
  104.0 41.0 reduce-scatter.5
  148.5 78.0 all-reduce.1
  230.4 84.9 all-gather.4
  319.9 147.0 reduce-scatter.9
  469.6 42.1 reduce-scatter.7
